TPU v7x, 32 devices: a whole 2x2x4 slice. The times are simulated.
32 devices in a mesh: seg: 8 (over z, x), head: 4 (over y, core).
Axes of the slice: x: 2, y: 2, z: 4, core: 2. Of those that a mesh axis runs over, the one named last changes fastest.
Arguments:
- q_heads: bfloat16 [6144, 2048], P('seg', 'head'), may hold values from -6 to 6
- k_heads: bfloat16 [6144, 2048], P('seg', 'head'), may hold values from -6 to 6
- v_heads: bfloat16 [6144, 2048], P('seg', 'head'), may hold values from -600 to 600
- log_decay: float32 [16, 6144], P('head', 'seg'), may hold values from -1 to 0
- parent: int32 [8], replicated, may hold values from -1 to 7, as said below
- norm_gain: float32 [2048], P('head'), may hold values from 0.1 to 1.9
- w_out: bfloat16 [2048, 6144], P('head'), may hold values from -0.125 to 0.125
Outputs:
- mixed: bfloat16 [6144, 6144], P(('seg', 'head'))
Inputs may be any that keep to these rules, and one draw needn't show every extreme that they name: A segment's parent is a root or a segment whose parent is a root; the tree has three levels, and the third is never empty.
All inputs are finite; a program needn't handle non-finite values.
Results may differ from a plain program's by a relative error of at most 0.0051.
Values sent between devices are 32-bit elements; how exact they have to be, the bound alone decides.
A program may use at most 128 MiB of HBM per device.

v0:
```python
import jax
import jax.numpy as jnp
from jax import lax
from jax.sharding import PartitionSpec as P


def per_device(q_heads, k_heads, v_heads, log_decay, parent, norm_gain, w_out):
    segment_len = q_heads.shape[0]
    head_count = log_decay.shape[0]
    head_width = q_heads.shape[1] // head_count
    queries = q_heads.reshape(segment_len, head_count, head_width)
    key_rows = k_heads.reshape(segment_len, head_count, head_width)
    values = v_heads.reshape(segment_len, head_count, head_width)
    running = jnp.cumsum(log_decay, axis=1)
    segment_total = running[:, -1]
    key_weight = jnp.exp(segment_total[:, None] - running)
    weighted = key_rows.astype(jnp.float32) * key_weight.T[:, :, None]
    local_state = jnp.einsum(
        "shd,she->hde", weighted, values.astype(jnp.float32), precision=lax.Precision.HIGHEST
    )
    scores = jnp.einsum("thd,shd->hts", queries, key_rows, preferred_element_type=jnp.float32)
    row_index = lax.broadcasted_iota(jnp.int32, (segment_len, segment_len), 0)
    col_index = lax.broadcasted_iota(jnp.int32, (segment_len, segment_len), 1)
    causal = row_index >= col_index
    log_gap = running[:, :, None] - running[:, None, :]
    decay_factor = jnp.where(causal[None], jnp.exp(jnp.minimum(log_gap, 0.0)), 0.0)
    weights = (scores * head_width ** (-0.5) * decay_factor).astype(jnp.bfloat16)
    within = jnp.einsum("hts,she->the", weights, values, preferred_element_type=jnp.float32)
    own_index = lax.axis_index("seg")
    parent_id = parent[own_index]
    grand_id = jnp.where(parent_id >= 0, parent[jnp.maximum(parent_id, 0)], -1)
    states = lax.all_gather(local_state[None], "seg", axis=0, tiled=True)
    totals = lax.all_gather(segment_total[None], "seg", axis=0, tiled=True)
    segment_ids = jnp.arange(states.shape[0], dtype=jnp.int32)
    is_parent = segment_ids == parent_id
    is_grand = segment_ids == grand_id
    parent_sum = jnp.sum(jnp.where(is_parent[:, None, None, None], states, 0.0), axis=0)
    grand_sum = jnp.sum(jnp.where(is_grand[:, None, None, None], states, 0.0), axis=0)
    parent_total = jnp.sum(jnp.where(is_parent[:, None], totals, 0.0), axis=0)
    parent_sum, grand_sum, parent_total = (parent_sum, grand_sum, parent_total)
    prefix = jnp.exp(parent_total)[:, None, None] * grand_sum + parent_sum
    prefix_term = (
        jnp.einsum(
            "thd,hde->the", queries.astype(jnp.float32), prefix, precision=lax.Precision.HIGHEST
        )
        * jnp.exp(running).T[:, :, None]
    )
    attention = (prefix_term + within).reshape(segment_len, head_count * head_width)
    squares = lax.psum(jnp.sum(attention * attention, axis=1), "head")
    total_features = head_count * head_width * lax.axis_size("head")
    inverse = 1.0 / jnp.sqrt(squares / total_features + 1e-06)
    normed = (attention * inverse[:, None] * norm_gain[None, :]).astype(jnp.bfloat16)
    mixed = lax.psum_scatter(
        jnp.dot(normed, w_out, preferred_element_type=jnp.float32),
        "head",
        scatter_dimension=0,
        tiled=True,
    )
    return mixed.astype(jnp.bfloat16)


def solution(mesh):
    return jax.shard_map(
        per_device,
        mesh=mesh,
        in_specs=(
            P("seg", "head"),
            P("seg", "head"),
            P("seg", "head"),
            P("head", "seg"),
            P(),
            P("head"),
            P("head", None),
        ),
        out_specs=P(("seg", "head"), None),
        check_vma=False,
    )
```

profile of v0, /device:TPU:0, one launch (start us, length us, event | category | flops | bytes accessed | tf_op | source)
XLA Modules:
  0.0 234.6 jit_solution(15167253058687618074)
XLA Ops:
  6.5 0.0 copy-start
  6.5 0.0 all-gather.4.cloned.1.call-start
  6.5 0.8 reshape.72
  7.3 1.1 reduce-window.6
  8.5 0.2 slice_reduce_fusion
  8.6 0.2 reduce-window.9
  8.8 0.1 add_bitcast_fusion
  8.9 0.2 slice_reduce_fusion.1
  9.1 0.1 exponential_bitcast_fusion.1
  9.2 0.0 copy-start.3
  9.2 0.0 copy-start.4
  9.2 1.4 copy.31
  10.6 1.4 copy.32
  12.0 1.7 fusion.6
  13.7 0.0 all-gather.4.cloned.1.call-update
  13.7 0.0 reduce-scatter.2.cloned.1.call-start
  13.8 0.0 copy-done.3
  13.8 0.6 dynamic_slice.6
  15.7 0.6 dynamic_slice.7
  16.2 0.0 copy-done.4
  16.2 0.6 dynamic-slice
  17.5 0.2 dynamic-update-slice
  17.7 23.5 %all-reduce = f32[32]{0:T(128)S(1)} all-reduce(f32[32]{0:T(128)S(1)} %dynamic-update-slice), channel_id=2, replica_groups=mesh['seg'=8,'head'=4] {'seg'}, use_global_device_ids=true, to_apply=%add | all-reduce | flops 32 | bytes 256
  41.2 0.1 reshape.78
  41.3 0.7 iota_compare_fusion.2
  41.9 0.1 select_reduce_fusion.2
  42.6 0.2 iota_compare_fusion
  42.8 0.0 copy-done
  42.8 5.6 %fusion = f32[4,768,128]{1,2,0:T(8,128)} fusion(bf16[768,4,128]{0,2,1:T(8,128)(2,1)S(1)} %bitcast.52, f32[4,768]{1,0:T(4,128)S(1)} %get-tuple-element.8, pred[768,768]{1,0:T(8,128)(4,1)S(1)} %iota_compare_fusion, bf16[768,4,128]{0,2,1:T(8,128)(2,1)S(1)} %bitcast.50, bf16[768,512]{1,0:T(8,128)(2,1)S(1)} %copy-done), kind=kOutput, calls=%fused_computation.1 | convolution fusion | flops 1222115328 | bytes 4534272 | tf_op jit(solution)/shard_map/hts,she->the/dot_general | solution.py:28
  48.3 17.5 %all-gather.4.cloned.1.call-done = f32[32,128,128]{2,1,0:T(8,128)} async-done(((f32[4,128,128]{2,1,0:T(8,128)}), f32[32,128,128]{2,1,0:T(8,128)}) %all-gather.4.cloned.1.call-update) | async-done | bytes 2097168 | tf_op jit(solution)/shard_map/all_gather | solution.py:32
  65.9 0.0 copy-start.1
  65.9 2.1 select_reduce_fusion.1
  68.0 0.0 copy-start.2
  68.0 0.0 copy-done.1
  68.0 1.1 multiply_reduce_fusion
  69.1 5.7 %psum.7 = f32[768]{0:T(1024)S(1)} all-reduce(f32[768]{0:T(1024)S(1)} %get-tuple-element.9), channel_id=1, replica_groups=mesh['seg'=8,'head'=4] {'head'}, use_global_device_ids=true, to_apply=%region_6.7 | all-reduce | flops 768 | bytes 6144 | tf_op jit(solution)/shard_map/psum | solution.py:49
  74.8 0.0 copy-done.2
  74.8 0.2 fusion.5
  75.0 11.9 %fusion.21 = f32[768,6144]{1,0:T(8,128)} fusion(bf16[768,512]{0,1:T(8,128)(2,1)S(1)} %fusion.5, bf16[512,6144]{1,0:T(8,128)(2,1)} %param.13), kind=kOutput, calls=%fused_computation.36 | convolution fusion | flops 4831838208 | bytes 25952256 | tf_op jit(solution)/shard_map/dot_general | solution.py:54
  86.9 0.0 reduce-scatter.2.cloned.1.call-update
  87.0 136.8 %reduce-scatter.2.cloned.1.call-done = f32[192,6144]{1,0:T(8,128)} async-done(((f32[768,6144]{1,0:T(8,128)}), f32[192,6144]{1,0:T(8,128)}) %reduce-scatter.2.cloned.1.call-update) | async-done | bytes 4718608 | tf_op jit(solution)/shard_map/reduce_scatter | solution.py:53
  223.7 4.1 %convert_element_type.17 = bf16[192,6144]{1,0:T(8,128)(2,1)} convert(f32[192,6144]{1,0:T(8,128)} %reduce-scatter.2.cloned.1.call-done) | non-fusion elementwise | flops 1179648 | bytes 7077888 | tf_op jit(solution)/shard_map/convert_element_type | solution.py:59
  (5 shorter events, 0.0 us)
Async XLA Ops:
  6.5 36.2 %copy-start = (bf16[768,512]{1,0:T(8,128)(2,1)S(1)}, bf16[768,512]{1,0:T(8,128)(2,1)}, u32[]{:S(2)}) copy-start(bf16[768,512]{1,0:T(8,128)(2,1)} %param.7) | copy-start | bytes 2359300
  6.5 59.3 %all-gather.4.cloned.1.call-start = ((), (), s32[]{:S(2)}) async-start(), calls=%async_computation.2 | async-start | bytes 2359296 | tf_op jit(solution)/shard_map/all_gather | solution.py:32
  9.2 4.6 %copy-start.3 = (s32[8]{0:T(128)S(1)}, s32[8]{0:T(128)}, u32[]{:S(2)}) copy-start(s32[8]{0:T(128)} %param.11) | copy-start | bytes 100
  9.2 7.1 %copy-start.4 = (u32[32]{0:T(128)S(1)}, u32[32]{0:T(128)}, u32[]{:S(2)}) copy-start(u32[32]{0:T(128)} %constant.29) | copy-start | bytes 388
  13.7 210.0 %reduce-scatter.2.cloned.1.call-start = ((), (), s32[]{:S(2)}) async-start(), calls=%async_computation.1 | async-start | bytes 23592960 | tf_op jit(solution)/shard_map/reduce_scatter | solution.py:53
  65.9 2.1 copy-start.1
  68.0 6.8 %copy-start.2 = (f32[512]{0:T(512)S(1)}, f32[512]{0:T(512)}, u32[]{:S(2)}) copy-start(f32[512]{0:T(512)} %param.12) | copy-start | bytes 6148
Sparse Core Ops, SparseCore 0:
  13.8 51.9 all-gather.3
  87.1 136.6 reduce-scatter.1
where the time goes:
time: 235 us
  waiting for transfers between devices  154 us (66%)
  blocking collectives  29.1 us (12%)
  matrix products  20.2 us (9%)
  between operations  16 us (7%)
  other arithmetic  8.75 us (4%)
  local copies, waits for them, and re-layouts  6.08 us (3%)
    reduce_scatter x1, waiting for transfers between devices, per_device(): lax.psum_scatter(jnp.dot(normed, w_out, preferred_element_type=jnp.float3...  137 us
    unnamed x1, blocking collectives  23.5 us
    all_gather x1, waiting for transfers between devices, per_device(): states = lax.all_gather(local_state[None], 'seg', axis=0, tiled=True)  17.5 us
    dot_general x1, matrix products, per_device(): jnp.dot(normed, w_out, preferred_element_type=jnp.float32)  11.9 us
    psum x1, blocking collectives, per_device(): squares = lax.psum(jnp.sum(attention * attention, axis=1), 'head')  5.67 us
    dot_general x1, matrix products, per_device(): jnp.einsum('hts,she->the', weights, values, preferred_element_type=jnp.fl...  5.55 us
  transfers between devices with their start and end apart: 2, of which 2 were waited for; matrix products, arithmetic and copies ran while one was open for 4% of the time, Pallas kernels for 0%

commit v1 on v0

--- a/solution.py
+++ b/solution.py
@@ -29,7 +29,14 @@
     own_index = lax.axis_index("seg")
     parent_id = parent[own_index]
     grand_id = jnp.where(parent_id >= 0, parent[jnp.maximum(parent_id, 0)], -1)
-    states = lax.all_gather(local_state[None], "seg", axis=0, tiled=True)
+    own = local_state[None]
+    devices = lax.axis_size("seg")
+    held, parts = (own, [own])
+    for _ in range(devices - 1):
+        held = lax.ppermute(held, "seg", [(i, (i + 1) % devices) for i in range(devices)])
+        parts.insert(0, held)
+    row_of_blocks = jnp.concatenate(parts, axis=0)
+    states = jnp.roll(row_of_blocks, (lax.axis_index("seg") + 1) * own.shape[0], axis=0)
     totals = lax.all_gather(segment_total[None], "seg", axis=0, tiled=True)
     segment_ids = jnp.arange(states.shape[0], dtype=jnp.int32)
     is_parent = segment_ids == parent_id

time: 235 us -> 271 us (1.15)
  waiting for transfers between devices: 154 us -> 184 us
  local copies, waits for them, and re-layouts: 6.08 us -> 12.1 us
  starting transfers between devices: 0.04 us -> 3.04 us
    ppermute x0 -> x7, waiting for transfers between devices: none -> 48.4 us  [per_device(): lax.ppermute(held, 'seg', [(i, (i + 1) % devices) for i in range(devices)])]
    all_gather x1 -> x0, waiting for transfers between devices: 17.5 us -> none  [per_device(): states = lax.all_gather(local_state[None], 'seg', axis=0, tiled=True)]
    unnamed x13 -> x32, local copies, waits for them, and re-layouts: 0.86 us -> 6.68 us
    ppermute x0 -> x7, starting transfers between devices: none -> 3.03 us  [per_device(): lax.ppermute(held, 'seg', [(i, (i + 1) % devices) for i in range(devices)])]
  transfers between devices with their start and end apart: 2 -> 8, of which waited for: 2 -> 7; matrix products, arithmetic and copies ran while one was open for 4% -> 4% of each run, Pallas kernels for 0% -> 0%
where the time goes in v1:
time: 271 us
  waiting for transfers between devices  184 us (68%)
  blocking collectives  27.5 us (10%)
  matrix products  20.6 us (8%)
  between operations  16.3 us (6%)
  local copies, waits for them, and re-layouts  12.1 us (4%)
  other arithmetic  7.85 us (3%)
  starting transfers between devices  3.04 us (1%)
    reduce_scatter x1, waiting for transfers between devices, per_device(): lax.psum_scatter(jnp.dot(normed, w_out, preferred_element_type=jnp.float3...  135 us
    ppermute x7, waiting for transfers between devices, per_device(): lax.ppermute(held, 'seg', [(i, (i + 1) % devices) for i in range(devices)])  48.4 us
    unnamed x1, blocking collectives  21.8 us
    dot_general x1, matrix products, per_device(): jnp.dot(normed, w_out, preferred_element_type=jnp.float32)  11.9 us
    unnamed x32, local copies, waits for them, and re-layouts  6.68 us
    dot_general x1, matrix products, per_device(): jnp.einsum('hts,she->the', weights, values, preferred_element_type=jnp.fl...  6.63 us
    psum x1, blocking collectives, per_device(): squares = lax.psum(jnp.sum(attention * attention, axis=1), 'head')  5.67 us
  transfers between devices with their start and end apart: 8, of which 7 were waited for; matrix products, arithmetic and copies ran while one was open for 4% of the time, Pallas kernels for 0%

profile of v1, /device:TPU:0, one launch (start us, length us, event | category | flops | bytes accessed | tf_op | source)
XLA Modules:
  0.0 270.9 jit_solution(12039541505339274029)
XLA Ops:
  6.5 0.8 reshape.72
  7.3 1.1 reduce-window.6
  8.5 0.2 slice_reduce_fusion
  8.6 0.2 reduce-window.9
  8.8 0.1 add_bitcast_fusion
  8.9 0.2 slice_reduce_fusion.1
  9.1 0.1 exponential_bitcast_fusion.1
  9.2 1.4 copy.31
  10.6 1.4 copy.32
  12.0 0.9 fusion.9
  12.9 3.0 %collective-permute-start = (f32[1,4,128,128]{3,2,1,0:T(8,128)S(1)}, f32[1,4,128,128]{3,2,1,0:T(8,128)S(1)}, u32[]{:S(2)}, u32[]{:S(2)}) collective-permute-start(f32[1,4,128,128]{3,2,1,0:T(8,128)S(1)} %fusion.9), channel_id=1, source_target_pairs={{0,4},{4,8},{8,12},{12,16},{16,20},{20,24},{24,28},{28,0},{1,5},{5... | collective-permute-start | bytes 786440 | tf_op jit(solution)/shard_map/ppermute | solution.py:36
  15.9 9.3 %collective-permute-done = f32[1,4,128,128]{3,2,1,0:T(8,128)S(1)} collective-permute-done((f32[1,4,128,128]{3,2,1,0:T(8,128)S(1)}, f32[1,4,128,128]{3,2,1,0:T(8,128)S(1)}, u32[]{:S(2)}, u32[]{:S(2)}) %collective-permute-start) | collective-permute-done | bytes 262176 | tf_op jit(solution)/shard_map/ppermute | solution.py:36
  25.3 0.0 collective-permute-start.1
  25.3 10.2 %collective-permute-done.1 = f32[1,4,128,128]{3,2,1,0:T(8,128)S(1)} collective-permute-done((f32[1,4,128,128]{3,2,1,0:T(8,128)S(1)}, f32[1,4,128,128]{3,2,1,0:T(8,128)S(1)}, u32[]{:S(2)}, u32[]{:S(2)}) %collective-permute-start.1) | collective-permute-done | bytes 262176 | tf_op jit(solution)/shard_map/ppermute | solution.py:36
  35.4 0.0 collective-permute-start.2
  35.4 9.3 %collective-permute-done.2 = f32[1,4,128,128]{3,2,1,0:T(8,128)S(1)} collective-permute-done((f32[1,4,128,128]{3,2,1,0:T(8,128)S(1)}, f32[1,4,128,128]{3,2,1,0:T(8,128)S(1)}, u32[]{:S(2)}, u32[]{:S(2)}) %collective-permute-start.2) | collective-permute-done | bytes 262176 | tf_op jit(solution)/shard_map/ppermute | solution.py:36
  44.8 0.0 collective-permute-start.3
  44.8 9.1 %collective-permute-done.3 = f32[1,4,128,128]{3,2,1,0:T(8,128)S(1)} collective-permute-done((f32[1,4,128,128]{3,2,1,0:T(8,128)S(1)}, f32[1,4,128,128]{3,2,1,0:T(8,128)S(1)}, u32[]{:S(2)}, u32[]{:S(2)}) %collective-permute-start.3) | collective-permute-done | bytes 262176 | tf_op jit(solution)/shard_map/ppermute | solution.py:36
  53.8 0.7 copy-done.2
  54.5 0.0 collective-permute-start.4
  54.5 1.0 iota_compare_fusion
  55.5 8.2 %collective-permute-done.4 = f32[1,4,128,128]{3,2,1,0:T(8,128)} collective-permute-done((f32[1,4,128,128]{3,2,1,0:T(8,128)S(1)}, f32[1,4,128,128]{3,2,1,0:T(8,128)}, u32[]{:S(2)}, u32[]{:S(2)}) %collective-permute-start.4) | collective-permute-done | bytes 262176 | tf_op jit(solution)/shard_map/ppermute | solution.py:36
  63.7 0.0 collective-permute-start.5
  63.7 6.6 %fusion = f32[4,768,128]{1,2,0:T(8,128)} fusion(bf16[768,4,128]{0,2,1:T(8,128)(2,1)S(1)} %bitcast.53, f32[4,768]{1,0:T(4,128)S(1)} %get-tuple-element.8, pred[768,768]{1,0:T(8,128)(4,1)} %iota_compare_fusion, bf16[768,4,128]{0,2,1:T(8,128)(2,1)S(1)} %bitcast.51, bf16[768,512]{1,0:T(8,128)(2,1)S(1)} %copy-done), kind=kOutput, calls=%fused_computation.1 | convolution fusion | flops 1222115328 | bytes 4534272 | tf_op jit(solution)/shard_map/hts,she->the/dot_general | solution.py:28
  70.3 0.7 dynamic_slice.10
  71.0 2.4 collective-permute-done.5
  73.4 0.7 iota_compare_fusion.2
  75.5 0.7 dynamic_slice.11
  76.1 0.6 dynamic-slice
  77.3 0.2 dynamic-update-slice
  77.5 21.8 %all-reduce = f32[32]{0:T(128)S(1)} all-reduce(f32[32]{0:T(128)S(1)} %dynamic-update-slice), channel_id=2, replica_groups=mesh['seg'=8,'head'=4] {'seg'}, use_global_device_ids=true, to_apply=%add | all-reduce | flops 32 | bytes 256
  99.4 0.1 reshape.78
  99.4 0.1 select_reduce_fusion.2
  100.3 1.0 constant_dynamic-update-slice_fusion.14
  101.3 1.0 constant_dynamic-update-slice_fusion.13
  102.2 1.0 constant_dynamic-update-slice_fusion.12
  103.2 0.0 copy-start.1
  103.4 1.1 constant_dynamic-update-slice_fusion.6
  104.4 1.0 constant_dynamic-update-slice_fusion.5
  105.5 0.0 copy-start.4
  105.6 0.4 select_reduce_fusion.1
  106.0 1.1 multiply_reduce_fusion
  107.1 5.7 %psum.7 = f32[768]{0:T(1024)S(1)} all-reduce(f32[768]{0:T(1024)S(1)} %get-tuple-element.9), channel_id=1, replica_groups=mesh['seg'=8,'head'=4] {'head'}, use_global_device_ids=true, to_apply=%region_6.7 | all-reduce | flops 768 | bytes 6144 | tf_op jit(solution)/shard_map/psum | solution.py:56
  112.7 0.2 fusion.5
  112.9 11.9 %fusion.24 = f32[768,6144]{1,0:T(8,128)} fusion(bf16[768,512]{0,1:T(8,128)(2,1)S(1)} %fusion.5, bf16[512,6144]{1,0:T(8,128)(2,1)} %param.13), kind=kOutput, calls=%fused_computation.53 | convolution fusion | flops 4831838208 | bytes 25952256 | tf_op jit(solution)/shard_map/dot_general | solution.py:61
  124.9 0.0 reduce-scatter.2.cloned.1.call-update
  124.9 135.1 %reduce-scatter.2.cloned.1.call-done = f32[192,6144]{1,0:T(8,128)} async-done(((f32[768,6144]{1,0:T(8,128)}), f32[192,6144]{1,0:T(8,128)}) %reduce-scatter.2.cloned.1.call-update) | async-done | bytes 4718608 | tf_op jit(solution)/shard_map/reduce_scatter | solution.py:60
  260.0 4.1 %convert_element_type.17 = bf16[192,6144]{1,0:T(8,128)(2,1)} convert(f32[192,6144]{1,0:T(8,128)} %reduce-scatter.2.cloned.1.call-done) | non-fusion elementwise | flops 1179648 | bytes 7077888 | tf_op jit(solution)/shard_map/convert_element_type | solution.py:66
  (30 shorter events, 0.3 us)
Async XLA Ops:
  6.5 57.2 %copy-start = (bf16[768,512]{1,0:T(8,128)(2,1)S(1)}, bf16[768,512]{1,0:T(8,128)(2,1)}, u32[]{:S(2)}) copy-start(bf16[768,512]{1,0:T(8,128)(2,1)} %param.7) | copy-start | bytes 2359300
  6.5 253.4 %reduce-scatter.2.cloned.1.call-start = ((), (), s32[]{:S(2)}) async-start(), calls=%async_computation.1 | async-start | bytes 23592960 | tf_op jit(solution)/shard_map/reduce_scatter | solution.py:60
  12.9 12.4 %collective-permute-start = (f32[1,4,128,128]{3,2,1,0:T(8,128)S(1)}, f32[1,4,128,128]{3,2,1,0:T(8,128)S(1)}, u32[]{:S(2)}, u32[]{:S(2)}) collective-permute-start(f32[1,4,128,128]{3,2,1,0:T(8,128)S(1)} %fusion.9), channel_id=1, source_target_pairs={{0,4},{4,8},{8,12},{12,16},{16,20},{20,24},{24,28},{28,0},{1,5},{5... | collective-permute-start | bytes 786440 | tf_op jit(solution)/shard_map/ppermute | solution.py:36
  25.3 10.2 %collective-permute-start.1 = (f32[1,4,128,128]{3,2,1,0:T(8,128)S(1)}, f32[1,4,128,128]{3,2,1,0:T(8,128)S(1)}, u32[]{:S(2)}, u32[]{:S(2)}) collective-permute-start(f32[1,4,128,128]{3,2,1,0:T(8,128)S(1)} %collective-permute-done), channel_id=1, source_target_pairs={{0,4},{4,8},{8,12},{12,16},{16,20},{20,24},{24,28},{28,0},{1,5},{5... | collective-permute-start | bytes 786440 | tf_op jit(solution)/shard_map/ppermute | solution.py:36
  35.4 9.3 %collective-permute-start.2 = (f32[1,4,128,128]{3,2,1,0:T(8,128)S(1)}, f32[1,4,128,128]{3,2,1,0:T(8,128)S(1)}, u32[]{:S(2)}, u32[]{:S(2)}) collective-permute-start(f32[1,4,128,128]{3,2,1,0:T(8,128)S(1)} %collective-permute-done.1), channel_id=1, source_target_pairs={{0,4},{4,8},{8,12},{12,16},{16,20},{20,24},{24,28},{28,0},{1,5},{5... | collective-permute-start | bytes 786440 | tf_op jit(solution)/shard_map/ppermute | solution.py:36
  44.8 9.1 %collective-permute-start.3 = (f32[1,4,128,128]{3,2,1,0:T(8,128)S(1)}, f32[1,4,128,128]{3,2,1,0:T(8,128)S(1)}, u32[]{:S(2)}, u32[]{:S(2)}) collective-permute-start(f32[1,4,128,128]{3,2,1,0:T(8,128)S(1)} %collective-permute-done.2), channel_id=1, source_target_pairs={{0,4},{4,8},{8,12},{12,16},{16,20},{20,24},{24,28},{28,0},{1,5},{5... | collective-permute-start | bytes 786440 | tf_op jit(solution)/shard_map/ppermute | solution.py:36
  53.8 0.7 copy-start.2
  54.5 9.2 %collective-permute-start.4 = (f32[1,4,128,128]{3,2,1,0:T(8,128)S(1)}, f32[1,4,128,128]{3,2,1,0:T(8,128)}, u32[]{:S(2)}, u32[]{:S(2)}) collective-permute-start(f32[1,4,128,128]{3,2,1,0:T(8,128)S(1)} %collective-permute-done.3), channel_id=1, source_target_pairs={{0,4},{4,8},{8,12},{12,16},{16,20},{20,24},{24,28},{28,0},{1,5},{5... | collective-permute-start | bytes 786440 | tf_op jit(solution)/shard_map/ppermute | solution.py:36
  55.5 14.8 %copy-start.5 = (s32[8]{0:T(128)S(1)}, s32[8]{0:T(128)}, u32[]{:S(2)}) copy-start(s32[8]{0:T(128)} %param.11) | copy-start | bytes 100
  55.5 20.6 %copy-start.6 = (u32[32]{0:T(128)S(1)}, u32[32]{0:T(128)}, u32[]{:S(2)}) copy-start(u32[32]{0:T(128)} %constant.51) | copy-start | bytes 388
  63.7 9.7 %collective-permute-start.5 = (f32[1,4,128,128]{3,2,1,0:T(8,128)}, f32[1,4,128,128]{3,2,1,0:T(8,128)}, u32[]{:S(2)}, u32[]{:S(2)}) collective-permute-start(f32[1,4,128,128]{3,2,1,0:T(8,128)} %collective-permute-done.4), channel_id=1, source_target_pairs={{0,4},{4,8},{8,12},{12,16},{16,20},{20,24},{24,28},{28,0},{1,5},{5... | collective-permute-start | bytes 786440 | tf_op jit(solution)/shard_map/ppermute | solution.py:36
  70.3 35.1 %copy-start.3 = (f32[1,4,128,128]{3,2,1,0:T(8,128)S(1)}, f32[1,4,128,128]{3,2,1,0:T(8,128)}, u32[]{:S(2)}) copy-start(f32[1,4,128,128]{3,2,1,0:T(8,128)} %copy-done.2) | copy-start | bytes 786436
  73.4 26.9 %collective-permute-start.6 = (f32[1,4,128,128]{3,2,1,0:T(8,128)}, f32[1,4,128,128]{3,2,1,0:T(8,128)S(1)}, u32[]{:S(2)}, u32[]{:S(2)}) collective-permute-start(f32[1,4,128,128]{3,2,1,0:T(8,128)} %collective-permute-done.5), channel_id=1, source_target_pairs={{0,4},{4,8},{8,12},{12,16},{16,20},{20,24},{24,28},{28,0},{1,5},{5... | collective-permute-start | bytes 786440 | tf_op jit(solution)/shard_map/ppermute | solution.py:36
  103.2 2.7 %copy-start.1 = (f32[4,768,128]{1,2,0:T(8,128)S(1)}, f32[4,768,128]{1,2,0:T(8,128)}, u32[]{:S(2)}) copy-start(f32[4,768,128]{1,2,0:T(8,128)} %fusion) | copy-start | bytes 4718596
  105.5 7.2 %copy-start.4 = (f32[512]{0:T(512)S(1)}, f32[512]{0:T(512)}, u32[]{:S(2)}) copy-start(f32[512]{0:T(512)} %param.12) | copy-start | bytes 6148
Sparse Core Ops, SparseCore 0:
  125.0 134.9 reduce-scatter.1
